TPU v7x, 256 devices: a whole 4x4x8 slice. The times are simulated.
256 devices in a mesh: seq: 64 (over x, z, core), ch: 4 (over y).
Axes of the slice: x: 4, y: 4, z: 8, core: 2. Of those that a mesh axis runs over, the one named last changes fastest.
Arguments:
- proj: bfloat16 [3, 128, 65536], P(None, 'ch', 'seq'), may hold values from -6 to 6
- cotangent: bfloat16 [128, 65536], P('ch', 'seq'), may hold values from -6 to 6
- short_w: float32 [3, 128, 3], P(None, 'ch'), may hold values from -3.5 to 3.5
- filter_in: float32 [32, 64], replicated, may hold values from -5 to 5
- filter_out: float32 [64, 128], P(None, 'ch'), may hold values from -0.75 to 0.75
- rates: float32 [128], P('ch'), may hold values from 0.25 to 2184
Outputs:
- grad_proj: bfloat16 [3, 128, 65536], P(None, 'ch', 'seq')
- grad_short: float32 [3, 128, 3], P(None, 'ch')
- grad_filter_out: float32 [64, 128], P(None, 'ch')
- grad_filter_in: float32 [32, 64], replicated
All inputs are finite; a program needn't handle non-finite values.
Results may differ from a plain program's by a relative error of at most 0.0013.
Values may be sent and summed in bfloat16 or wider, within the bound.
A program may use at most 64 MiB of HBM per device.

v0:
```python
import math
import jax
import jax.numpy as jnp
from jax import lax
from jax.sharding import PartitionSpec as P

PRECISE = lax.Precision.HIGHEST


def shifted(value, axis, by):
    length = lax.axis_size(axis)
    pairs = [(i, i + by) for i in range(length) if 0 <= i + by < length]
    return lax.ppermute(value, axis, pairs)


def position_features(positions, length, feature_count):
    feature_index = jnp.arange(feature_count, dtype=jnp.int32)
    multiplier = (1 + feature_index // 2 * 499) % length
    upper = positions // 1024
    lower = positions % 1024
    phases = (
        upper[:, None] * (multiplier * 1024 % length)[None, :]
        + lower[:, None] * multiplier[None, :]
    ) % length
    angles = phases.astype(jnp.float32) * (2.0 * math.pi / length)
    return jnp.where((feature_index % 2 == 0)[None, :], jnp.cos(angles), jnp.sin(angles))


def angle_tables(row_count, col_count, row_start, col_start, modulus):
    row_index = row_start + jnp.arange(row_count, dtype=jnp.int32)
    col_index = col_start + jnp.arange(col_count, dtype=jnp.int32)
    phases = row_index[:, None] * col_index[None, :] % modulus
    angles = phases.astype(jnp.float32) * (2.0 * math.pi / modulus)
    return (jnp.cos(angles), jnp.sin(angles))


def rotate(real_part, imag_part, cosine, sine, sign):
    return (
        real_part * cosine - sign * imag_part * sine,
        imag_part * cosine + sign * real_part * sine,
    )


def dft_axis(real_part, imag_part, form, cosine, sine, sign):
    real_cos = jnp.einsum(form, real_part, cosine, precision=PRECISE)
    real_sin = jnp.einsum(form, real_part, sine, precision=PRECISE)
    imag_cos = jnp.einsum(form, imag_part, cosine, precision=PRECISE)
    imag_sin = jnp.einsum(form, imag_part, sine, precision=PRECISE)
    return (real_cos - sign * imag_sin, imag_cos + sign * real_sin)


def shards(proj, cotangent, short_w, filter_in, filter_out, rates):
    tap_count = short_w.shape[2]
    channels = proj.shape[1]
    devices = lax.axis_size("seq")
    tokens_here = proj.shape[2]
    length = devices * tokens_here
    modulus = 2 * length
    norm_scale = 1.0 / math.sqrt(length)
    column_width = tokens_here // devices
    first_split = math.gcd(tokens_here, 64)
    second_split = tokens_here // first_split
    device_index = lax.axis_index("seq")
    rim_cols = shifted(proj[:, :, tokens_here - (tap_count - 1) :], "seq", 1)
    extended = jnp.concatenate([rim_cols, proj], 2).astype(jnp.float32)

    def delayed(offset):
        return extended[:, :, tap_count - 1 - offset : tap_count - 1 - offset + tokens_here]

    mixed_all = short_w[:, :, 0, None] * delayed(0)
    for offset in range(1, tap_count):
        mixed_all = mixed_all + short_w[:, :, offset, None] * delayed(offset)
    query_part, key_part, value_part = (mixed_all[0], mixed_all[1], mixed_all[2])
    gated_prod = key_part * value_part
    cotangent_full = cotangent.astype(jnp.float32)
    grad_conv = cotangent_full * query_part
    both_signals = jnp.concatenate([gated_prod, grad_conv], 0).reshape(2 * channels, 1, tokens_here)
    columns = lax.all_to_all(both_signals, "seq", split_axis=2, concat_axis=1, tiled=True)
    block_start = jnp.arange(devices, dtype=jnp.int32) * tokens_here
    offset_start = device_index * column_width + jnp.arange(column_width, dtype=jnp.int32)
    column_pos = (block_start[:, None] + offset_start[None, :]).reshape(devices * column_width)
    features = position_features(column_pos, length, filter_in.shape[0])
    preact = jnp.dot(features, filter_in, precision=PRECISE, preferred_element_type=jnp.float32)
    hidden = jnp.sin(preact)
    modulated = jnp.einsum("to,oc->ct", hidden, filter_out, precision=PRECISE)
    relative = column_pos.astype(jnp.float32) / length
    spread = jnp.sqrt(jnp.expm1(-2.0 * rates) / jnp.expm1(-2.0 * rates / length))
    envelope = jnp.exp(-rates[:, None] * relative[None, :]) / spread[:, None]
    kernel = (envelope * modulated).reshape(channels, devices, column_width)
    stacked = jnp.concatenate([columns[:channels], kernel, columns[channels:]], 0)
    cos_outer, sin_outer = angle_tables(devices, 2 * devices, 0, 0, 2 * devices)
    turned_real = jnp.einsum("ran,ak->rkn", stacked, cos_outer, precision=PRECISE)
    turned_imag = -jnp.einsum("ran,ak->rkn", stacked, sin_outer, precision=PRECISE)
    cos_turn, sin_turn = angle_tables(
        2 * devices, column_width, 0, device_index * column_width, modulus
    )
    turned_real, turned_imag = rotate(turned_real, turned_imag, cos_turn, sin_turn, -1.0)
    moved_real, moved_imag = (
        lax.all_to_all(turned_real, "seq", split_axis=1, concat_axis=2, tiled=True),
        lax.all_to_all(turned_imag, "seq", split_axis=1, concat_axis=2, tiled=True),
    )
    row_total = moved_real.shape[0]
    cos_first, sin_first = angle_tables(first_split, first_split, 0, 0, first_split)
    cos_second, sin_second = angle_tables(second_split, second_split, 0, 0, second_split)
    cos_mid, sin_mid = angle_tables(first_split, second_split, 0, 0, tokens_here)
    grid_real = moved_real.reshape(row_total, 2, first_split, second_split)
    grid_imag = moved_imag.reshape(row_total, 2, first_split, second_split)
    grid_real, grid_imag = dft_axis(
        grid_real, grid_imag, "rkab,ac->rkcb", cos_first, sin_first, -1.0
    )
    grid_real, grid_imag = rotate(grid_real, grid_imag, cos_mid, sin_mid, -1.0)
    spec_real, spec_imag = dft_axis(
        grid_real, grid_imag, "rkcb,bd->rkcd", cos_second, sin_second, -1.0
    )
    gated_real, gated_imag = (spec_real[:channels], spec_imag[:channels])
    kernel_real, kernel_imag = (
        spec_real[channels : 2 * channels],
        spec_imag[channels : 2 * channels],
    )
    grad_real, grad_imag = (spec_real[2 * channels :], spec_imag[2 * channels :])
    conv_real = gated_real * kernel_real - gated_imag * kernel_imag
    conv_imag = gated_real * kernel_imag + gated_imag * kernel_real
    back_real = grad_real * kernel_real + grad_imag * kernel_imag
    back_imag = grad_imag * kernel_real - grad_real * kernel_imag
    kgrad_real = grad_real * gated_real + grad_imag * gated_imag
    kgrad_imag = grad_imag * gated_real - grad_real * gated_imag
    cos_back, sin_back = angle_tables(2, tokens_here, 2 * device_index, 0, modulus)
    cos_last, sin_last = angle_tables(2 * devices, devices, 0, 0, 2 * devices)
    real_part = jnp.concatenate([conv_real, back_real, kgrad_real], 0)
    rows = real_part.shape[0]
    part_real, part_imag = dft_axis(
        real_part,
        jnp.concatenate([conv_imag, back_imag, kgrad_imag], 0),
        "rkcd,db->rkcb",
        cos_second,
        sin_second,
        1.0,
    )
    part_real, part_imag = rotate(part_real, part_imag, cos_mid, sin_mid, 1.0)
    part_real, part_imag = dft_axis(
        part_real, part_imag, "rkcb,ca->rkab", cos_first, sin_first, 1.0
    )
    part_real = part_real.reshape(rows, 2, tokens_here)
    part_imag = part_imag.reshape(rows, 2, tokens_here)
    part_real, part_imag = rotate(part_real, part_imag, cos_back[None], sin_back[None], 1.0)
    spread_real = lax.all_to_all(part_real, "seq", split_axis=2, concat_axis=1, tiled=True)
    spread_imag = lax.all_to_all(part_imag, "seq", split_axis=2, concat_axis=1, tiled=True)
    real_out = jnp.einsum("rkn,ka->ran", spread_real, cos_last, precision=PRECISE)
    real_out = (real_out - jnp.einsum("rkn,ka->ran", spread_imag, sin_last, precision=PRECISE)) * (
        1.0 / modulus
    )
    conv_cols = real_out[:channels]
    gated_cols = real_out[channels : 2 * channels]
    kernel_grad = real_out[2 * channels :]
    returned = lax.all_to_all(
        jnp.concatenate([conv_cols, gated_cols], 0), "seq", split_axis=1, concat_axis=2, tiled=True
    )
    returned = returned.reshape(2 * channels, tokens_here)
    conv_out = returned[:channels]
    grad_gated = returned[channels:]
    grad_mixed = jnp.stack(
        [cotangent_full * conv_out, grad_gated * value_part, grad_gated * key_part]
    )
    short_part = jnp.stack(
        [jnp.sum(grad_mixed * delayed(offset), axis=2) for offset in range(tap_count)], axis=2
    )
    weighted = envelope * kernel_grad.reshape(channels, devices * column_width)
    out_part = jnp.einsum("to,ct->oc", hidden, weighted, precision=PRECISE)
    grad_hidden = jnp.einsum("ct,oc->to", weighted, filter_out, precision=PRECISE)
    in_part = jnp.einsum("tf,to->fo", features, grad_hidden * jnp.cos(preact), precision=PRECISE)
    next_rim = shifted(grad_mixed[:, :, : tap_count - 1], "seq", -1)
    grad_extended = jnp.concatenate([grad_mixed, next_rim], 2)
    result = short_w[:, :, 0, None] * grad_extended[:, :, 0:tokens_here]
    for offset in range(1, tap_count):
        result = (
            result
            + short_w[:, :, offset, None] * grad_extended[:, :, offset : offset + tokens_here]
        )
    grad_proj = result.astype(jnp.bfloat16)
    short_total, out_total = lax.psum((short_part, out_part), "seq")
    in_total = lax.psum(in_part, ("seq", "ch"))
    return (grad_proj, short_total * norm_scale, out_total * norm_scale, in_total * norm_scale)


def solution(mesh):
    placed = (
        P(None, "ch", "seq"),
        P("ch", "seq"),
        P(None, "ch", None),
        P(),
        P(None, "ch"),
        P("ch"),
    )
    return jax.shard_map(
        shards,
        mesh=mesh,
        in_specs=placed,
        out_specs=(P(None, "ch", "seq"), P(None, "ch", None), P(None, "ch"), P()),
        check_vma=False,
    )
```

profile of v0, /device:TPU:8, one launch (start us, length us, event | category | flops | bytes accessed | tf_op | source)
XLA Modules:
  0.0 598.5 jit_solution(10087766709720511439)
XLA Ops:
  4.3 5.1 fusion.244
  12.4 3.8 reduce
  16.2 2.1 reshape.320
  18.3 13.3 %all-to-all-start = ((f32[64,1,1024]{2,1,0:T(1,128)}), f32[64,1,1024]{2,1,0:T(1,128)}, u32[]{:S(2)}, u32[]{:S(2)}) async-start(f32[64,1,1024]{2,1,0:T(1,128)} %reshape.320), calls=%async_computation | async-start | bytes 524288 | tf_op jit(solution)/shard_map/all_to_all | solution.py:78
  37.6 5.8 all-to-all-done
  43.4 2.9 reduce.1
  46.4 2.4 reshape.321
  48.8 2.3 fusion.241
  53.9 2.9 add_bitcast_fusion.1
  56.9 2.5 copy.152
  59.4 6.3 %all-to-all-start.2 = ((f32[96,128,16]{0,2,1:T(8,128)}), f32[96,128,16]{0,2,1:T(8,128)}, u32[]{:S(2)}, u32[]{:S(2)}) async-start(f32[96,128,16]{0,2,1:T(8,128)} %copy.152), calls=%async_computation.2 | async-start | bytes 2097152 | tf_op jit(solution)/shard_map/all_to_all | solution.py:100
  65.6 2.5 copy.150
  68.2 25.5 %all-to-all-done.2 = f32[96,128,16]{0,2,1:T(8,128)} async-done(((f32[96,128,16]{0,2,1:T(8,128)}), f32[96,128,16]{0,2,1:T(8,128)}, u32[]{:S(2)}, u32[]{:S(2)}) %all-to-all-start.2) | async-done | bytes 786464 | tf_op jit(solution)/shard_map/all_to_all | solution.py:100
  93.7 7.2 %all-to-all-start.1 = ((f32[96,128,16]{0,2,1:T(8,128)}), f32[96,128,16]{0,2,1:T(8,128)}, u32[]{:S(2)}, u32[]{:S(2)}) async-start(f32[96,128,16]{0,2,1:T(8,128)} %copy.150), calls=%async_computation.1 | async-start | bytes 2097152 | tf_op jit(solution)/shard_map/all_to_all | solution.py:99
  101.4 3.8 fusion.14
  105.3 23.3 %all-to-all-done.1 = f32[96,128,16]{0,2,1:T(8,128)} async-done(((f32[96,128,16]{0,2,1:T(8,128)}), f32[96,128,16]{0,2,1:T(8,128)}, u32[]{:S(2)}, u32[]{:S(2)}) %all-to-all-start.1) | async-done | bytes 786464 | tf_op jit(solution)/shard_map/all_to_all | solution.py:99
  128.5 2.9 fusion.18
  131.5 2.9 fusion.7
  134.4 3.4 subtract_bitcast_fusion
  163.5 6.8 %all-to-all-start.3 = ((f32[96,2,1024]{0,1,2:T(2,128)}), f32[96,2,1024]{0,1,2:T(2,128)}, u32[]{:S(2)}, u32[]{:S(2)}) async-start(f32[96,2,1024]{0,1,2:T(2,128)} %copy.166), calls=%async_computation.3 | async-start | bytes 2097152 | tf_op jit(solution)/shard_map/all_to_all | solution.py:146
  170.4 3.0 copy.170
  173.4 25.0 %all-to-all-done.3 = f32[96,2,1024]{0,1,2:T(2,128)} async-done(((f32[96,2,1024]{0,1,2:T(2,128)}), f32[96,2,1024]{0,1,2:T(2,128)}, u32[]{:S(2)}, u32[]{:S(2)}) %all-to-all-start.3) | async-done | bytes 786464 | tf_op jit(solution)/shard_map/all_to_all | solution.py:146
  198.4 6.8 %all-to-all-start.4 = ((f32[96,2,1024]{0,1,2:T(2,128)}), f32[96,2,1024]{0,1,2:T(2,128)}, u32[]{:S(2)}, u32[]{:S(2)}) async-start(f32[96,2,1024]{0,1,2:T(2,128)} %copy.170), calls=%async_computation.4 | async-start | bytes 2097152 | tf_op jit(solution)/shard_map/all_to_all | solution.py:147
  208.5 24.7 %all-to-all-done.4 = f32[96,2,1024]{0,1,2:T(2,128)} async-done(((f32[96,2,1024]{0,1,2:T(2,128)}), f32[96,2,1024]{0,1,2:T(2,128)}, u32[]{:S(2)}, u32[]{:S(2)}) %all-to-all-start.4) | async-done | bytes 786464 | tf_op jit(solution)/shard_map/all_to_all | solution.py:147
  238.8 2.1 reshape.322
  240.9 7.0 %all-to-all-start.5 = ((f32[64,1,1024]{2,1,0:T(1,128)}), f32[64,1,1024]{2,1,0:T(1,128)}, u32[]{:S(2)}, u32[]{:S(2)}) async-start(f32[64,1,1024]{2,1,0:T(1,128)} %reshape.322), calls=%async_computation.5 | async-start | bytes 524288 | tf_op jit(solution)/shard_map/all_to_all | solution.py:155
  247.8 2.2 copy.175
  251.9 2.2 convolution_multiply_fusion.4
  254.1 3.0 fusion.43
  257.1 75.9 %psum.23 = f32[32,64]{1,0:T(8,128)S(1)} all-reduce(f32[32,64]{1,0:T(8,128)S(1)} %fusion.43), channel_id=1, replica_groups=mesh['seq'=64,'ch'=4] {'seq','ch'}, use_global_device_ids=true, to_apply=%region_5.6 | all-reduce | flops 2048 | bytes 16384 | tf_op jit(solution)/shard_map/psum | solution.py:181
  334.4 2.9 reduce.2
  346.4 250.5 %all-reduce = (f32[3,32,3]{1,0,2:T(4,128)S(1)}, f32[64,32]{0,1:T(8,128)S(1)}) all-reduce(f32[3,32,3]{1,0,2:T(4,128)S(1)} %pad_maximum_fusion.7, f32[64,32]{0,1:T(8,128)S(1)} %fusion.238), channel_id=1, replica_groups=mesh['seq'=64,'ch'=4] {'seq'}, use_global_device_ids=true, to_apply=%region_3.4 | all-reduce | flops 2336 | bytes 18688 | tf_op jit(solution)/shard_map/psum | solution.py:180
  (110 shorter events, 63.7 us)
Async XLA Ops:
  0.6 3.7 copy-start
  0.6 8.8 %copy-start.6 = (bf16[32,1024]{1,0:T(8,128)(2,1)S(1)}, bf16[32,1024]{1,0:T(8,128)(2,1)}, u32[]{:S(2)}) copy-start(bf16[32,1024]{1,0:T(8,128)(2,1)} %param.7) | copy-start | bytes 196612
  1.5 8.1 %collective-permute-start = (bf16[3,32,2]{2,1,0:T(8,128)(2,1)S(1)}, bf16[3,32,2]{2,1,0:T(8,128)(2,1)S(1)}, u32[]{:S(2)}, u32[]{:S(2)}) collective-permute-start(bf16[3,32,2]{2,1,0:T(8,128)(2,1)S(1)} %slice.96), channel_id=1, source_target_pairs={{0,4},{4,8},{8,12},{12,16},{16,20},{20,24},{24,28},{28,32},{32,36}... | collective-permute-start | bytes 1160 | tf_op jit(solution)/shard_map/ppermute | solution.py:13
  3.3 6.3 %copy-start.10 = (s32[32]{0:T(128)}, s32[32]{0:T(128)S(1)}, u32[]{:S(2)}) copy-start(s32[32]{0:T(128)S(1)} %get-tuple-element.66) | copy-start | bytes 388
  3.3 6.3 %copy-start.12 = (pred[32]{0:T(512)(128)(4,1)}, pred[32]{0:T(512)(128)(4,1)S(1)}, u32[]{:S(2)}) copy-start(pred[32]{0:T(512)(128)(4,1)S(1)} %fusion.143) | copy-start | bytes 100
  4.3 5.3 copy-start.5
  11.9 19.7 %copy-start.9 = (f32[32]{0:T(128)S(1)}, f32[32]{0:T(128)}, u32[]{:S(2)}) copy-start(f32[32]{0:T(128)} %param.11) | copy-start | bytes 388
  11.9 19.7 %copy-start.7 = (f32[64,32]{0,1:T(8,128)S(1)}, f32[64,32]{0,1:T(8,128)}, u32[]{:S(2)}) copy-start(f32[64,32]{0,1:T(8,128)} %param.10) | copy-start | bytes 24580
  18.3 25.2 %all-to-all-start = ((f32[64,1,1024]{2,1,0:T(1,128)}), f32[64,1,1024]{2,1,0:T(1,128)}, u32[]{:S(2)}, u32[]{:S(2)}) async-start(f32[64,1,1024]{2,1,0:T(1,128)} %reshape.320), calls=%async_computation | async-start | bytes 524288 | tf_op jit(solution)/shard_map/all_to_all | solution.py:78
  51.1 1.0 copy-start.2
  59.4 34.3 %all-to-all-start.2 = ((f32[96,128,16]{0,2,1:T(8,128)}), f32[96,128,16]{0,2,1:T(8,128)}, u32[]{:S(2)}, u32[]{:S(2)}) async-start(f32[96,128,16]{0,2,1:T(8,128)} %copy.152), calls=%async_computation.2 | async-start | bytes 2097152 | tf_op jit(solution)/shard_map/all_to_all | solution.py:100
  93.7 34.9 %all-to-all-start.1 = ((f32[96,128,16]{0,2,1:T(8,128)}), f32[96,128,16]{0,2,1:T(8,128)}, u32[]{:S(2)}, u32[]{:S(2)}) async-start(f32[96,128,16]{0,2,1:T(8,128)} %copy.150), calls=%async_computation.1 | async-start | bytes 2097152 | tf_op jit(solution)/shard_map/all_to_all | solution.py:99
  128.5 3.0 copy-start.3
  163.5 34.9 %all-to-all-start.3 = ((f32[96,2,1024]{0,1,2:T(2,128)}), f32[96,2,1024]{0,1,2:T(2,128)}, u32[]{:S(2)}, u32[]{:S(2)}) async-start(f32[96,2,1024]{0,1,2:T(2,128)} %copy.166), calls=%async_computation.3 | async-start | bytes 2097152 | tf_op jit(solution)/shard_map/all_to_all | solution.py:146
  198.4 34.9 %all-to-all-start.4 = ((f32[96,2,1024]{0,1,2:T(2,128)}), f32[96,2,1024]{0,1,2:T(2,128)}, u32[]{:S(2)}, u32[]{:S(2)}) async-start(f32[96,2,1024]{0,1,2:T(2,128)} %copy.170), calls=%async_computation.4 | async-start | bytes 2097152 | tf_op jit(solution)/shard_map/all_to_all | solution.py:147
  234.5 1.0 copy-start.4
  238.8 13.1 %copy-start.8 = (f32[64,32]{0,1:T(8,128)S(1)}, f32[64,32]{0,1:T(8,128)}, u32[]{:S(2)}) copy-start(f32[64,32]{0,1:T(8,128)} %param.10) | copy-start | bytes 24580
  240.9 13.2 %copy-start.11 = (s32[32]{0:T(128)S(1)}, s32[32]{0:T(128)}, u32[]{:S(2)}) copy-start(s32[32]{0:T(128)} %copy-done.10) | copy-start | bytes 388
  240.9 13.2 %copy-start.13 = (pred[32]{0:T(512)(128)(4,1)S(1)}, pred[32]{0:T(512)(128)(4,1)}, u32[]{:S(2)}) copy-start(pred[32]{0:T(512)(128)(4,1)} %copy-done.12) | copy-start | bytes 100
  240.9 93.6 %all-to-all-start.5 = ((f32[64,1,1024]{2,1,0:T(1,128)}), f32[64,1,1024]{2,1,0:T(1,128)}, u32[]{:S(2)}, u32[]{:S(2)}) async-start(f32[64,1,1024]{2,1,0:T(1,128)} %reshape.322), calls=%async_computation.5 | async-start | bytes 524288 | tf_op jit(solution)/shard_map/all_to_all | solution.py:155
  341.0 3.1 collective-permute-start.1
  344.1 253.9 %copy-start.1 = (f32[32,64]{1,0:T(8,128)S(1)}, f32[32,64]{1,0:T(8,128)}, u32[]{:S(2)}) copy-start(f32[32,64]{1,0:T(8,128)} %param.9) | copy-start | bytes 24580
where the time goes:
time: 605 us; the launch traced here: 599 us
  blocking collectives  326 us (54%)
  waiting for transfers between devices  106 us (18%)
  matrix products  52.9 us (9%)
  starting transfers between devices  50.4 us (8%)
  local copies, waits for them, and re-layouts  42.8 us (7%)
  other arithmetic  18.9 us (3%)
    psum x1, blocking collectives, shards(): short_total, out_total = lax.psum((short_part, out_part), 'seq')  250 us
    psum x1, blocking collectives, shards(): in_total = lax.psum(in_part, ('seq', 'ch'))  75.9 us
    all_to_all x1, waiting for transfers between devices, shards(): lax.all_to_all(turned_imag, 'seq', split_axis=1, concat_axis=2, tiled=True)  25.5 us
    all_to_all x1, waiting for transfers between devices, shards(): lax.all_to_all(part_real, 'seq', split_axis=2, concat_axis=1, tiled=True)  25 us
    all_to_all x1, waiting for transfers between devices, shards(): lax.all_to_all(part_imag, 'seq', split_axis=2, concat_axis=1, tiled=True)  24.7 us
    all_to_all x1, waiting for transfers between devices, shards(): lax.all_to_all(turned_real, 'seq', split_axis=1, concat_axis=2, tiled=True)  23.3 us
    all_to_all x1, starting transfers between devices, shards(): lax.all_to_all(both_signals, 'seq', split_axis=2, concat_axis=1, tiled=True)  13.3 us
    unnamed x38, local copies, waits for them, and re-layouts  12.3 us
  transfers between devices with their start and end apart: 8, of which 6 were waited for; matrix products, arithmetic and copies ran while one was open for 6% of the time, Pallas kernels for 0%

commit v1 on v0

--- a/solution.py
+++ b/solution.py
@@ -178,7 +178,9 @@
         )
     grad_proj = result.astype(jnp.bfloat16)
     short_total, out_total = lax.psum((short_part, out_part), "seq")
-    in_total = lax.psum(in_part, ("seq", "ch"))
+    in_total = in_part
+    for h in ("ch", "seq"):
+        in_total = jax.lax.psum(in_total, h)
     return (grad_proj, short_total * norm_scale, out_total * norm_scale, in_total * norm_scale)
 
 

time: 605 us -> 544 us (0.90)
  blocking collectives: 326 us -> 261 us
    psum x1, blocking collectives: 75.9 us -> 14.1 us  [shards(): in_total = jax.lax.psum(in_total, h)]
    unnamed x38 -> x50, local copies, waits for them, and re-layouts: 12.3 us -> 14.4 us
  transfers between devices with their start and end apart: 8 -> 8, of which waited for: 6 -> 6; matrix products, arithmetic and copies ran while one was open for 6% -> 7% of each run, Pallas kernels for 0% -> 0%
where the time goes in v1:
time: 544 us; the launch traced here: 537 us
  blocking collectives  261 us (48%)
  waiting for transfers between devices  106 us (19%)
  matrix products  52 us (10%)
  starting transfers between devices  50.4 us (9%)
  local copies, waits for them, and re-layouts  44.8 us (8%)
  other arithmetic  21 us (4%)
    psum x1, blocking collectives, shards(): short_total, out_total = lax.psum((short_part, out_part), 'seq')  246 us
    all_to_all x1, waiting for transfers between devices, shards(): lax.all_to_all(turned_imag, 'seq', split_axis=1, concat_axis=2, tiled=True)  25.5 us
    all_to_all x1, waiting for transfers between devices, shards(): lax.all_to_all(part_real, 'seq', split_axis=2, concat_axis=1, tiled=True)  25 us
    all_to_all x1, waiting for transfers between devices, shards(): lax.all_to_all(part_imag, 'seq', split_axis=2, concat_axis=1, tiled=True)  24.7 us
    all_to_all x1, waiting for transfers between devices, shards(): lax.all_to_all(turned_real, 'seq', split_axis=1, concat_axis=2, tiled=True)  23.3 us
    unnamed x50, local copies, waits for them, and re-layouts  14.4 us
    psum x1, blocking collectives, shards(): in_total = jax.lax.psum(in_total, h)  14.1 us
    all_to_all x1, starting transfers between devices, shards(): lax.all_to_all(both_signals, 'seq', split_axis=2, concat_axis=1, tiled=True)  13.3 us
  transfers between devices with their start and end apart: 8, of which 6 were waited for; matrix products, arithmetic and copies ran while one was open for 7% of the time, Pallas kernels for 0%

profile of v1, /device:TPU:8, one launch (start us, length us, event | category | flops | bytes accessed | tf_op | source)
XLA Modules:
  0.0 537.0 jit_solution(1288926309835482088)
XLA Ops:
  4.3 5.1 fusion.244
  12.4 3.8 reduce
  18.3 13.3 %all-to-all-start = ((f32[64,1,1024]{2,1,0:T(1,128)}), f32[64,1,1024]{2,1,0:T(1,128)}, u32[]{:S(2)}, u32[]{:S(2)}) async-start(f32[64,1,1024]{2,1,0:T(1,128)} %reshape.320), calls=%async_computation | async-start | bytes 524288 | tf_op jit(solution)/shard_map/all_to_all | solution.py:78
  37.6 5.8 %all-to-all-done = f32[64,1,1024]{2,1,0:T(1,128)} async-done(((f32[64,1,1024]{2,1,0:T(1,128)}), f32[64,1,1024]{2,1,0:T(1,128)}, u32[]{:S(2)}, u32[]{:S(2)}) %all-to-all-start) | async-done | bytes 262176 | tf_op jit(solution)/shard_map/all_to_all | solution.py:78
  43.5 2.9 reduce.1
  46.4 2.4 reshape.321
  48.9 2.3 fusion.241
  54.0 2.9 add_bitcast_fusion.1
  56.9 2.5 copy.152
  59.4 6.3 %all-to-all-start.2 = ((f32[96,128,16]{0,2,1:T(8,128)}), f32[96,128,16]{0,2,1:T(8,128)}, u32[]{:S(2)}, u32[]{:S(2)}) async-start(f32[96,128,16]{0,2,1:T(8,128)} %copy.152), calls=%async_computation.2 | async-start | bytes 2097152 | tf_op jit(solution)/shard_map/all_to_all | solution.py:100
  65.7 2.5 copy.150
  68.2 25.5 %all-to-all-done.2 = f32[96,128,16]{0,2,1:T(8,128)} async-done(((f32[96,128,16]{0,2,1:T(8,128)}), f32[96,128,16]{0,2,1:T(8,128)}, u32[]{:S(2)}, u32[]{:S(2)}) %all-to-all-start.2) | async-done | bytes 786464 | tf_op jit(solution)/shard_map/all_to_all | solution.py:100
  93.7 7.2 %all-to-all-start.1 = ((f32[96,128,16]{0,2,1:T(8,128)}), f32[96,128,16]{0,2,1:T(8,128)}, u32[]{:S(2)}, u32[]{:S(2)}) async-start(f32[96,128,16]{0,2,1:T(8,128)} %copy.150), calls=%async_computation.1 | async-start | bytes 2097152 | tf_op jit(solution)/shard_map/all_to_all | solution.py:99
  101.5 3.8 fusion.14
  105.3 23.3 %all-to-all-done.1 = f32[96,128,16]{0,2,1:T(8,128)} async-done(((f32[96,128,16]{0,2,1:T(8,128)}), f32[96,128,16]{0,2,1:T(8,128)}, u32[]{:S(2)}, u32[]{:S(2)}) %all-to-all-start.1) | async-done | bytes 786464 | tf_op jit(solution)/shard_map/all_to_all | solution.py:99
  128.6 2.9 fusion.18
  131.5 2.9 fusion.7
  134.5 3.4 subtract_bitcast_fusion
  163.6 6.8 %all-to-all-start.3 = ((f32[96,2,1024]{0,1,2:T(2,128)}), f32[96,2,1024]{0,1,2:T(2,128)}, u32[]{:S(2)}, u32[]{:S(2)}) async-start(f32[96,2,1024]{0,1,2:T(2,128)} %copy.166), calls=%async_computation.3 | async-start | bytes 2097152 | tf_op jit(solution)/shard_map/all_to_all | solution.py:146
  170.4 3.0 copy.170
  173.4 25.0 %all-to-all-done.3 = f32[96,2,1024]{0,1,2:T(2,128)} async-done(((f32[96,2,1024]{0,1,2:T(2,128)}), f32[96,2,1024]{0,1,2:T(2,128)}, u32[]{:S(2)}, u32[]{:S(2)}) %all-to-all-start.3) | async-done | bytes 786464 | tf_op jit(solution)/shard_map/all_to_all | solution.py:146
  198.4 6.8 %all-to-all-start.4 = ((f32[96,2,1024]{0,1,2:T(2,128)}), f32[96,2,1024]{0,1,2:T(2,128)}, u32[]{:S(2)}, u32[]{:S(2)}) async-start(f32[96,2,1024]{0,1,2:T(2,128)} %copy.170), calls=%async_computation.4 | async-start | bytes 2097152 | tf_op jit(solution)/shard_map/all_to_all | solution.py:147
  208.6 24.7 %all-to-all-done.4 = f32[96,2,1024]{0,1,2:T(2,128)} async-done(((f32[96,2,1024]{0,1,2:T(2,128)}), f32[96,2,1024]{0,1,2:T(2,128)}, u32[]{:S(2)}, u32[]{:S(2)}) %all-to-all-start.4) | async-done | bytes 786464 | tf_op jit(solution)/shard_map/all_to_all | solution.py:147
  238.8 2.1 reshape.322
  240.9 7.0 %all-to-all-start.5 = ((f32[64,1,1024]{2,1,0:T(1,128)}), f32[64,1,1024]{2,1,0:T(1,128)}, u32[]{:S(2)}, u32[]{:S(2)}) async-start(f32[64,1,1024]{2,1,0:T(1,128)} %reshape.322), calls=%async_computation.5 | async-start | bytes 524288 | tf_op jit(solution)/shard_map/all_to_all | solution.py:155
  247.9 2.2 copy.175
  251.9 2.3 convolution_multiply_fusion.4
  254.2 3.0 fusion.43
  259.7 2.9 reduce.2
  268.4 14.1 %psum.30 = f32[32,64]{1,0:T(8,128)S(1)} all-reduce(f32[32,64]{1,0:T(8,128)S(1)} %fusion.43), channel_id=1, replica_groups=mesh['seq'=64,'ch'=4] {'ch'}, use_global_device_ids=true, to_apply=%region_5.6 | all-reduce | flops 2048 | bytes 16384 | tf_op jit(solution)/shard_map/psum | solution.py:183
  284.1 2.1 multiply_reduce_fusion.2
  288.2 246.5 %all-reduce = (f32[3,32,3]{1,0,2:T(4,128)S(1)}, f32[64,32]{0,1:T(8,128)S(1)}, f32[32,64]{1,0:T(8,128)S(1)}) all-reduce(f32[3,32,3]{1,0,2:T(4,128)S(1)} %pad_maximum_fusion.7, f32[64,32]{0,1:T(8,128)S(1)} %fusion.238, f32[32,64]{1,0:T(8,128)S(1)} %psum.30), channel_id=1, replica_groups=mesh['seq'=64,'ch'=4] {'seq'}, use_global_device_ids=true, to_apply=%region_3.4 | all-reduce | flops 4384 | bytes 35072 | tf_op jit(solution)/shard_map/psum | solution.py:180
  (122 shorter events, 67.7 us)
Async XLA Ops:
  0.6 3.7 copy-start
  0.6 8.8 %copy-start.11 = (bf16[32,1024]{1,0:T(8,128)(2,1)S(1)}, bf16[32,1024]{1,0:T(8,128)(2,1)}, u32[]{:S(2)}) copy-start(bf16[32,1024]{1,0:T(8,128)(2,1)} %param.7) | copy-start | bytes 196612
  1.5 8.2 %collective-permute-start = (bf16[3,32,2]{2,1,0:T(8,128)(2,1)S(1)}, bf16[3,32,2]{2,1,0:T(8,128)(2,1)S(1)}, u32[]{:S(2)}, u32[]{:S(2)}) collective-permute-start(bf16[3,32,2]{2,1,0:T(8,128)(2,1)S(1)} %slice.96), channel_id=1, source_target_pairs={{0,4},{4,8},{8,12},{12,16},{16,20},{20,24},{24,28},{28,32},{32,36}... | collective-permute-start | bytes 1160 | tf_op jit(solution)/shard_map/ppermute | solution.py:13
  3.3 6.4 %copy-start.15 = (s32[32]{0:T(128)}, s32[32]{0:T(128)S(1)}, u32[]{:S(2)}) copy-start(s32[32]{0:T(128)S(1)} %get-tuple-element.67) | copy-start | bytes 388
  3.3 6.3 %copy-start.17 = (pred[32]{0:T(512)(128)(4,1)}, pred[32]{0:T(512)(128)(4,1)S(1)}, u32[]{:S(2)}) copy-start(pred[32]{0:T(512)(128)(4,1)S(1)} %fusion.143) | copy-start | bytes 100
  4.3 5.3 copy-start.9
  11.9 19.7 %copy-start.14 = (f32[32]{0:T(128)S(1)}, f32[32]{0:T(128)}, u32[]{:S(2)}) copy-start(f32[32]{0:T(128)} %param.11) | copy-start | bytes 388
  11.9 19.8 %copy-start.12 = (f32[64,32]{0,1:T(8,128)S(1)}, f32[64,32]{0,1:T(8,128)}, u32[]{:S(2)}) copy-start(f32[64,32]{0,1:T(8,128)} %param.10) | copy-start | bytes 24580
  18.3 25.2 %all-to-all-start = ((f32[64,1,1024]{2,1,0:T(1,128)}), f32[64,1,1024]{2,1,0:T(1,128)}, u32[]{:S(2)}, u32[]{:S(2)}) async-start(f32[64,1,1024]{2,1,0:T(1,128)} %reshape.320), calls=%async_computation | async-start | bytes 524288 | tf_op jit(solution)/shard_map/all_to_all | solution.py:78
  51.2 1.0 copy-start.6
  59.4 34.3 %all-to-all-start.2 = ((f32[96,128,16]{0,2,1:T(8,128)}), f32[96,128,16]{0,2,1:T(8,128)}, u32[]{:S(2)}, u32[]{:S(2)}) async-start(f32[96,128,16]{0,2,1:T(8,128)} %copy.152), calls=%async_computation.2 | async-start | bytes 2097152 | tf_op jit(solution)/shard_map/all_to_all | solution.py:100
  93.7 34.9 %all-to-all-start.1 = ((f32[96,128,16]{0,2,1:T(8,128)}), f32[96,128,16]{0,2,1:T(8,128)}, u32[]{:S(2)}, u32[]{:S(2)}) async-start(f32[96,128,16]{0,2,1:T(8,128)} %copy.150), calls=%async_computation.1 | async-start | bytes 2097152 | tf_op jit(solution)/shard_map/all_to_all | solution.py:99
  128.6 3.0 copy-start.7
  163.6 34.9 %all-to-all-start.3 = ((f32[96,2,1024]{0,1,2:T(2,128)}), f32[96,2,1024]{0,1,2:T(2,128)}, u32[]{:S(2)}, u32[]{:S(2)}) async-start(f32[96,2,1024]{0,1,2:T(2,128)} %copy.166), calls=%async_computation.3 | async-start | bytes 2097152 | tf_op jit(solution)/shard_map/all_to_all | solution.py:146
  198.4 34.9 %all-to-all-start.4 = ((f32[96,2,1024]{0,1,2:T(2,128)}), f32[96,2,1024]{0,1,2:T(2,128)}, u32[]{:S(2)}, u32[]{:S(2)}) async-start(f32[96,2,1024]{0,1,2:T(2,128)} %copy.170), calls=%async_computation.4 | async-start | bytes 2097152 | tf_op jit(solution)/shard_map/all_to_all | solution.py:147
  234.6 1.0 copy-start.8
  238.8 13.1 %copy-start.13 = (f32[64,32]{0,1:T(8,128)S(1)}, f32[64,32]{0,1:T(8,128)}, u32[]{:S(2)}) copy-start(f32[64,32]{0,1:T(8,128)} %param.10) | copy-start | bytes 24580
  240.9 13.3 %copy-start.16 = (s32[32]{0:T(128)S(1)}, s32[32]{0:T(128)}, u32[]{:S(2)}) copy-start(s32[32]{0:T(128)} %copy-done.15) | copy-start | bytes 388
  240.9 13.3 %copy-start.18 = (pred[32]{0:T(512)(128)(4,1)S(1)}, pred[32]{0:T(512)(128)(4,1)}, u32[]{:S(2)}) copy-start(pred[32]{0:T(512)(128)(4,1)} %copy-done.17) | copy-start | bytes 100
  240.9 18.8 %all-to-all-start.5 = ((f32[64,1,1024]{2,1,0:T(1,128)}), f32[64,1,1024]{2,1,0:T(1,128)}, u32[]{:S(2)}, u32[]{:S(2)}) async-start(f32[64,1,1024]{2,1,0:T(1,128)} %reshape.322), calls=%async_computation.5 | async-start | bytes 524288 | tf_op jit(solution)/shard_map/all_to_all | solution.py:155
  251.9 5.3 copy-start.10
  251.9 5.3 copy-start.19
  266.1 0.8 copy-start.2
  266.1 1.0 copy-start.4
  267.1 15.4 %collective-permute-start.1 = (f32[3,32,2]{1,2,0:T(2,128)S(1)}, f32[3,32,2]{1,2,0:T(2,128)S(1)}, u32[]{:S(2)}, u32[]{:S(2)}) collective-permute-start(f32[3,32,2]{1,2,0:T(2,128)S(1)} %slice.139), channel_id=1, source_target_pairs={{4,0},{8,4},{12,8},{16,12},{20,16},{24,20},{28,24},{32,28},{36,32}... | collective-permute-start | bytes 2312 | tf_op jit(solution)/shard_map/ppermute | solution.py:13
  282.5 1.4 copy-start.3
  282.5 1.5 copy-start.5
  284.1 252.5 %copy-start.1 = (f32[32,64]{1,0:T(8,128)S(1)}, f32[32,64]{1,0:T(8,128)}, u32[]{:S(2)}) copy-start(f32[32,64]{1,0:T(8,128)} %param.9) | copy-start | bytes 24580
